TPU v7x, 128 devices: a whole 4x4x4 slice. The times are simulated.
128 devices in a mesh: grp: 4 (over x_hi, core), dom: 32 (over z, y, x_lo).
Axes of the slice: x: 4 (x_hi: 2, x_lo: 2; x = x_hi * 2 + x_lo), y: 4, z: 4, core: 2. Of those that a mesh axis runs over, the one named last changes fastest.
Arguments:
- nodes: bfloat16 [131072, 256], P(('grp', 'dom')), may hold values from -8 to 8
- neighbours: int32 [131072, 8], P(('grp', 'dom')), may hold values from 0 to 1279
- send_rows: int32 [32768], P(('grp', 'dom')), may hold values from 0 to 1023
- landmark_ids: int32 [8192], P(('grp', 'dom')), may hold values from 0 to 1023
- w_dst: bfloat16 [256, 256], replicated, may hold values from -0.375 to 0.375
- w_src: bfloat16 [256, 256], replicated, may hold values from -0.375 to 0.375
- w_msg: bfloat16 [256, 256], replicated, may hold values from -0.375 to 0.375
- edge_bias: float32 [256], replicated, may hold values from -4 to 4
- w_query: bfloat16 [256, 256], replicated, may hold values from -0.375 to 0.375
- w_key: bfloat16 [256, 256], replicated, may hold values from -0.375 to 0.375
- w_value: bfloat16 [256, 256], replicated, may hold values from -0.375 to 0.375
- w_out: bfloat16 [256, 256], replicated, may hold values from -0.375 to 0.375
Outputs:
- result: bfloat16 [131072, 256], P(('grp', 'dom'))
- kernel_term: float32 [131072, 256], P(('grp', 'dom'))
Inputs may be any that keep to these rules, and one draw needn't show every extreme that they name: `neighbours`: entries index the device's own 1024 rows, then the 128 rows received from the previous partition, then the 128 rows from the next one. `send_rows`: each partition's entries are rows of its own nodes. `landmark_ids`: each partition's entries are rows of its own nodes.
All inputs are finite; a program needn't handle non-finite values.
Results may differ from a plain program's by a relative error of at most 0.0054.
Values may be sent and summed in bfloat16 or wider, within the bound.
A program may use at most 64 MiB of HBM per device.

v0:
```python
import math
import jax
import jax.numpy as jnp
from jax import lax
from jax.sharding import PartitionSpec as P


def extended_2(cells, sides, width):
    for axis, dim in sides:
        count = lax.axis_size(axis)
        head = lax.slice_in_dim(cells, 0, width, axis=dim)
        tail = lax.slice_in_dim(cells, cells.shape[dim] - width, cells.shape[dim], axis=dim)
        cells = jnp.concatenate(
            [
                lax.ppermute(tail, axis, [(i, (i + 1) % count) for i in range(count)]),
                cells,
                lax.ppermute(head, axis, [((i + 1) % count, i) for i in range(count)]),
            ],
            axis=dim,
        )
    return cells


def rms_scale(values):
    return values * lax.rsqrt(jnp.mean(values * values, axis=-1, keepdims=True) + 1e-06)


def kernel_tile(query, key_rows):
    scale = 2.0 * query.shape[1] ** (-0.5)
    return jnp.exp(jnp.dot(query, key_rows.T, preferred_element_type=jnp.float32) * scale).astype(
        jnp.bfloat16
    )


def partial_sums(query, value, key_rows):
    total_rows = key_rows.shape[0]
    block_size = math.gcd(total_rows, 512)
    blocks = key_rows.reshape(total_rows // block_size, block_size, key_rows.shape[1])

    def partial_one_block(block_keys):
        kernel = kernel_tile(query, block_keys)
        return lax.dot_general(
            kernel, value, (((0,), (0,)), ((), ())), preferred_element_type=jnp.float32
        )

    return lax.map(partial_one_block, blocks).reshape(total_rows, value.shape[1])


def apply_sums(query, key_rows, sum_rows):
    total_rows = key_rows.shape[0]
    block_size = math.gcd(total_rows, 512)
    key_blocks = key_rows.reshape(total_rows // block_size, block_size, key_rows.shape[1])
    sum_blocks = sum_rows.reshape(total_rows // block_size, block_size, sum_rows.shape[1])

    def apply_one_block(accum, pair):
        block_keys, block_sums = pair
        kernel = kernel_tile(query, block_keys)
        return (accum + jnp.dot(kernel, block_sums, preferred_element_type=jnp.float32), None)

    start_value = jnp.zeros((query.shape[0], sum_rows.shape[1]), jnp.float32)
    accum, _ = lax.scan(apply_one_block, start_value, (key_blocks, sum_blocks))
    return accum


def shards(
    nodes,
    neighbours,
    send_rows,
    landmark_ids,
    w_dst,
    w_src,
    w_msg,
    edge_bias,
    w_query,
    w_key,
    w_value,
    w_out,
):
    halo_count = send_rows.shape[0] // 2
    outgoing = jnp.concatenate(
        [nodes[send_rows[:halo_count]], nodes[send_rows[halo_count:]]], axis=0
    )
    padded = extended_2(outgoing, ((("grp", "dom"), 0),), halo_count)
    extended = jnp.concatenate([nodes, padded[:halo_count], padded[3 * halo_count :]], axis=0)
    source = jnp.dot(extended, w_src, preferred_element_type=jnp.float32)
    target = jnp.dot(nodes, w_dst, preferred_element_type=jnp.float32)
    preact = target[:, None, :] + source[neighbours] + edge_bias
    messages = jnp.mean(jax.nn.gelu(preact), axis=1).astype(jnp.bfloat16)
    updated = (
        nodes.astype(jnp.float32) + jnp.dot(messages, w_msg, preferred_element_type=jnp.float32)
    ).astype(jnp.bfloat16)
    normed = rms_scale(updated.astype(jnp.float32)).astype(jnp.bfloat16)
    query = jnp.dot(normed, w_query, preferred_element_type=jnp.float32).astype(jnp.bfloat16)
    value = jnp.dot(normed, w_value, preferred_element_type=jnp.float32).astype(jnp.bfloat16)
    local_keys = jnp.dot(normed[landmark_ids], w_key, preferred_element_type=jnp.float32).astype(
        jnp.bfloat16
    )
    all_keys = lax.all_gather(local_keys, ("grp", "dom"), axis=0, tiled=True)
    own_sums = partial_sums(query, value, all_keys)
    total_sums = lax.psum(own_sums, ("grp", "dom")).astype(jnp.bfloat16)
    smooth = apply_sums(query, all_keys, total_sums)
    kernel_term = rms_scale(smooth)
    scaled = kernel_term.astype(jnp.bfloat16)
    result = updated.astype(jnp.float32) + jnp.dot(
        scaled, w_out, preferred_element_type=jnp.float32
    )
    return (result.astype(jnp.bfloat16), kernel_term)


def solution(mesh):
    return jax.shard_map(
        shards,
        mesh=mesh,
        in_specs=(
            P(("grp", "dom"), None),
            P(("grp", "dom"), None),
            P(("grp", "dom")),
            P(("grp", "dom")),
            P(),
            P(),
            P(),
            P(),
            P(),
            P(),
            P(),
            P(),
        ),
        out_specs=(P(("grp", "dom"), None), P(("grp", "dom"), None)),
        check_vma=False,
    )
```

profile of v0, /device:TPU:0, one launch (start us, length us, event | category | flops | bytes accessed | tf_op | source)
XLA Modules:
  0.0 572.5 jit_solution(5054479233434508780)
XLA Ops:
  7.2 0.0 all-gather.2.cloned.1.call-start
  7.2 0.8 compare_select_fusion.3
  8.0 1.9 gather_fusion
  9.9 1.6 collective-permute-start
  11.5 1.9 gather_fusion.1
  13.4 6.7 %collective-permute-start.1 = (bf16[128,256]{1,0:T(8,128)(2,1)S(1)}, bf16[128,256]{1,0:T(8,128)(2,1)}, u32[]{:S(2)}, u32[]{:S(2)}) collective-permute-start(bf16[128,256]{1,0:T(8,128)(2,1)S(1)} %gather_fusion.1), channel_id=1, source_target_pairs={{1,0},{2,1},{3,2},{4,3},{5,4},{6,5},{7,6},{8,7},{9,8},{10,9},{11,1... | collective-permute-start | bytes 196616 | tf_op jit(solution)/shard_map/ppermute | solution.py:17
  20.1 1.2 copy.18
  21.4 0.8 compare_select_fusion
  22.1 0.2 copy.19
  22.3 0.3 reshape.53
  22.6 1.4 fusion.46
  24.0 0.7 compare_select_fusion.1
  24.6 0.6 copy-done.7
  25.3 1.4 fusion.36
  26.7 31.6 %gather_fusion.2 = f32[8192,256]{1,0:T(8,128)} fusion(f32[1280,256]{1,0:T(8,128)S(1)} %fusion.36, s32[8192]{0:T(1024)S(1)} %broadcast_clamp_fusion), kind=kCustom, calls=%fused_computation.2 | custom fusion | bytes 16809984 | tf_op jit(solution)/shard_map/gather | solution.py:87
  58.3 7.8 %fusion.30 = f32[1024,256]{1,0:T(8,128)S(1)} fusion(f32[8192,256]{1,0:T(8,128)} %gather_fusion.2, f32[256]{0:T(256)S(1)} %copy-done.8, f32[1024,256]{1,0:T(8,128)S(1)} %fusion.46), kind=kLoop, calls=%fused_computation.31 | loop fusion | flops 22806528 | bytes 10486784 | tf_op jit(solution)/shard_map/reduce_sum | solution.py:88
  66.2 0.4 fusion.34
  66.6 0.1 fusion.35
  66.7 0.2 copy.20
  66.9 0.7 gather_fusion.3
  67.6 0.8 convolution_convert_fusion.2
  68.4 0.0 all-gather.2.cloned.1.call-update
  68.5 0.4 convolution_convert_fusion.1
  68.8 0.4 convolution_convert_fusion
  69.2 302.4 %all-gather.2.cloned.1.call-done = bf16[8192,256]{1,0:T(8,128)(2,1)} async-done(((bf16[64,256]{1,0:T(8,128)(2,1)}), bf16[8192,256]{1,0:T(8,128)(2,1)}) %all-gather.2.cloned.1.call-update) | async-done | bytes 4194320 | tf_op jit(solution)/shard_map/all_gather | solution.py:98
  371.6 41.7 %while.21 = (s32[]{:T(128)}, f32[16,512,256]{2,1,0:T(8,128)}, bf16[16,512,256]{2,1,0:T(8,128)(2,1)}, bf16[1024,256]{1,0:T(8,128)(2,1)S(1)}, bf16[1024,256]{1,0:T(8,128)(2,1)S(1)}, /*index=5*/s32[]{:T(128)}) while((s32[]{:T(128)}, f32[16,512,256]{2,1,0:T(8,128)}, bf16[16,512,256]{2,1,0:T(8,128)(2,1)}, bf16[1024,256]{1,0:T(8,128)(2,1)S(1)}, ...), condition=%wide.region_3.4_spmd, body=%wide.region_2.3_spmd.sunk | while | flops 537919488 | bytes 1836101 | solution.py:46
  371.6 2.6 fusion.72
  374.2 2.6 fusion.72
  376.8 2.6 fusion.72
  379.4 2.6 fusion.72
  382.0 2.6 fusion.72
  384.6 2.6 fusion.72
  387.2 2.6 fusion.72
  389.8 2.6 fusion.72
  392.4 2.6 fusion.72
  395.0 2.6 fusion.72
  397.6 2.6 fusion.72
  400.2 2.6 fusion.72
  402.8 2.6 fusion.72
  405.4 2.6 fusion.72
  408.0 2.6 fusion.72
  410.6 2.6 fusion.72
  413.3 114.5 %all-reduce.1 = bf16[8192,256]{1,0:T(8,128)(2,1)} all-reduce(f32[8192,256]{1,0:T(8,128)} %bitcast.52), channel_id=1, replica_groups=mesh['grp'=4,'dom'=32] {'grp','dom'}, use_global_device_ids=true, to_apply=%region_4.5 | all-reduce | flops 2097152 | bytes 12582912 | tf_op jit(solution)/shard_map/psum | solution.py:100
  527.7 36.1 %while.22 = (s32[]{:T(128)}, f32[1024,256]{1,0:T(8,128)S(1)}, bf16[16,512,256]{2,1,0:T(8,128)(2,1)}, bf16[1024,256]{1,0:T(8,128)(2,1)S(1)}, bf16[16,512,256]{2,1,0:T(8,128)(2,1)}, /*index=5*/s32[]{:T(128)}, s32[]{:T(128)}) while((s32[]{:T(128)}, f32[1024,256]{1,0:T(8,128)S(1)}, bf16[16,512,256]{2,1,0:T(8,128)(2,1)}, ...), condition=%wide.region_6.7_spmd.clone, body=%wide.region_5.6_spmd.clone.sunk | while | flops 538443776 | bytes 3146839 | solution.py:61
  527.7 2.3 fusion.76
  530.0 2.2 fusion.76
  532.3 2.2 fusion.76
  534.5 2.2 fusion.76
  536.8 2.2 fusion.76
  539.0 2.2 fusion.76
  541.3 2.2 fusion.76
  543.5 2.2 fusion.76
  545.8 2.2 fusion.76
  548.0 2.2 fusion.76
  550.3 2.2 fusion.76
  552.5 2.2 fusion.76
  554.8 2.2 fusion.76
  557.1 2.2 fusion.76
  559.3 2.2 fusion.76
  561.6 2.2 fusion.76
  563.8 0.2 multiply_reduce_fusion
  564.0 0.2 broadcast_multiply_fusion
  564.3 0.3 fusion.32
  564.6 1.0 copy.22
  (27 shorter events, 0.1 us)
Async XLA Ops:
  7.2 18.1 %copy-start = (bf16[256,256]{1,0:T(8,128)(2,1)S(1)}, bf16[256,256]{1,0:T(8,128)(2,1)}, u32[]{:S(2)}) copy-start(bf16[256,256]{1,0:T(8,128)(2,1)} %param.21) | copy-start | bytes 393220
  7.2 364.4 %all-gather.2.cloned.1.call-start = ((), (), s32[]{:S(2)}) async-start(), calls=%async_computation | async-start | bytes 4227072 | tf_op jit(solution)/shard_map/all_gather | solution.py:98
  9.9 14.8 %collective-permute-start = (bf16[128,256]{1,0:T(8,128)(2,1)S(1)}, bf16[128,256]{1,0:T(8,128)(2,1)S(1)}, u32[]{:S(2)}, u32[]{:S(2)}) collective-permute-start(bf16[128,256]{1,0:T(8,128)(2,1)S(1)} %gather_fusion), channel_id=1, source_target_pairs={{0,1},{1,2},{2,3},{3,4},{4,5},{5,6},{6,7},{7,8},{8,9},{9,10},{10,1... | collective-permute-start | bytes 196616 | tf_op jit(solution)/shard_map/ppermute | solution.py:15
  13.4 11.9 %collective-permute-start.1 = (bf16[128,256]{1,0:T(8,128)(2,1)S(1)}, bf16[128,256]{1,0:T(8,128)(2,1)}, u32[]{:S(2)}, u32[]{:S(2)}) collective-permute-start(bf16[128,256]{1,0:T(8,128)(2,1)S(1)} %gather_fusion.1), channel_id=1, source_target_pairs={{1,0},{2,1},{3,2},{4,3},{5,4},{6,5},{7,6},{8,7},{9,8},{10,9},{11,1... | collective-permute-start | bytes 196616 | tf_op jit(solution)/shard_map/ppermute | solution.py:17
  24.6 0.6 copy-start.7
  26.7 31.6 %copy-start.8 = (f32[256]{0:T(256)S(1)}, f32[256]{0:T(256)}, u32[]{:S(2)}) copy-start(f32[256]{0:T(256)} %param.23) | copy-start | bytes 3076
  58.3 7.9 %copy-start.2 = (bf16[256,256]{1,0:T(8,128)(2,1)S(1)}, bf16[256,256]{1,0:T(8,128)(2,1)}, u32[]{:S(2)}) copy-start(bf16[256,256]{1,0:T(8,128)(2,1)} %param.22) | copy-start | bytes 393220
  58.3 9.3 %copy-start.6 = (bf16[256,256]{1,0:T(8,128)(2,1)S(1)}, bf16[256,256]{1,0:T(8,128)(2,1)}, u32[]{:S(2)}) copy-start(bf16[256,256]{1,0:T(8,128)(2,1)} %param.25) | copy-start | bytes 393220
  58.3 10.1 %copy-start.3 = (bf16[256,256]{1,0:T(8,128)(2,1)S(1)}, bf16[256,256]{1,0:T(8,128)(2,1)}, u32[]{:S(2)}) copy-start(bf16[256,256]{1,0:T(8,128)(2,1)} %param.24) | copy-start | bytes 393220
  58.3 10.5 %copy-start.4 = (bf16[256,256]{1,0:T(8,128)(2,1)S(1)}, bf16[256,256]{1,0:T(8,128)(2,1)}, u32[]{:S(2)}) copy-start(bf16[256,256]{1,0:T(8,128)(2,1)} %param.26) | copy-start | bytes 393220
  527.7 36.5 %copy-start.5 = (bf16[256,256]{1,0:T(8,128)(2,1)S(1)}, bf16[256,256]{1,0:T(8,128)(2,1)}, u32[]{:S(2)}) copy-start(bf16[256,256]{1,0:T(8,128)(2,1)} %param.27) | copy-start | bytes 393220
  564.3 1.4 copy-start.1
Sparse Core Ops, SparseCore 0:
  68.6 302.9 all-gather.1
where the time goes:
time: 574 us; the launch traced here: 572 us
  waiting for transfers between devices  302 us (53%)
  blocking collectives  114 us (20%)
  matrix products  82.4 us (14%)
  local copies, waits for them, and re-layouts  39.6 us (7%)
  between operations  14.3 us (2%)
  other arithmetic  10.6 us (2%)
  starting transfers between devices  8.41 us (1%)
    all_gather x1, waiting for transfers between devices, shards(): all_keys = lax.all_gather(local_keys, ('grp', 'dom'), axis=0, tiled=True)  302 us
    psum x1, blocking collectives, shards(): total_sums = lax.psum(own_sums, ('grp', 'dom')).astype(jnp.bfloat16)  114 us
    dot_general x16, matrix products, partial_one_block(): lax.dot_general(kernel, value, (((0,), (0,)), ((), ())), preferred_elemen...  41.7 us
    dot_general x16, matrix products, apply_one_block(): jnp.dot(kernel, block_sums, preferred_element_type=jnp.float32)  35.7 us
    gather x1, local copies, waits for them, and re-layouts, shards(): preact = target[:, None, :] + source[neighbours] + edge_bias  31.6 us
  transfers between devices with their start and end apart: 3, of which 1 were waited for; matrix products, arithmetic and copies ran while one was open for 1% of the time, Pallas kernels for 0%

commit v1 on v0

--- a/solution.py
+++ b/solution.py
@@ -95,7 +95,12 @@
     local_keys = jnp.dot(normed[landmark_ids], w_key, preferred_element_type=jnp.float32).astype(
         jnp.bfloat16
     )
-    all_keys = lax.all_gather(local_keys, ("grp", "dom"), axis=0, tiled=True)
+    all_keys = jnp.concatenate(
+        lax.all_to_all(
+            jnp.stack([local_keys] * lax.axis_size(("grp", "dom"))), ("grp", "dom"), 0, 0
+        ),
+        axis=0,
+    )
     own_sums = partial_sums(query, value, all_keys)
     total_sums = lax.psum(own_sums, ("grp", "dom")).astype(jnp.bfloat16)
     smooth = apply_sums(query, all_keys, total_sums)

time: 574 us -> 315 us (0.55)
  waiting for transfers between devices: 302 us -> 52 us
  between operations: 14.3 us -> 0.88 us
  starting transfers between devices: 8.41 us -> 15 us
    all_gather x1 -> x0, waiting for transfers between devices: 302 us -> none  [shards(): all_keys = lax.all_gather(local_keys, ('grp', 'dom'), axis=0, tiled=True)]
    all_to_all x0 -> x1, waiting for transfers between devices: none -> 52 us  [shards(): lax.all_to_all(jnp.stack([local_keys] * lax.axis_size(('grp', 'dom'))), (...]
    all_to_all x0 -> x1, starting transfers between devices: none -> 6.61 us  [shards(): lax.all_to_all(jnp.stack([local_keys] * lax.axis_size(('grp', 'dom'))), (...]
  transfers between devices with their start and end apart: 3 -> 3, of which waited for: 1 -> 1; matrix products, arithmetic and copies ran while one was open for 1% -> 2% of each run, Pallas kernels for 0% -> 0%
where the time goes in v1:
time: 315 us; the launch traced here: 314 us
  blocking collectives  111 us (35%)
  matrix products  81.7 us (26%)
  waiting for transfers between devices  52 us (17%)
  local copies, waits for them, and re-layouts  41.9 us (13%)
  starting transfers between devices  15 us (5%)
  other arithmetic  10.5 us (3%)
    psum x1, blocking collectives, shards(): total_sums = lax.psum(own_sums, ('grp', 'dom')).astype(jnp.bfloat16)  111 us
    all_to_all x1, waiting for transfers between devices, shards(): lax.all_to_all(jnp.stack([local_keys] * lax.axis_size(('grp', 'dom'))), (...  52 us
    dot_general x16, matrix products, partial_one_block(): lax.dot_general(kernel, value, (((0,), (0,)), ((), ())), preferred_elemen...  41.6 us
    dot_general x16, matrix products, apply_one_block(): jnp.dot(kernel, block_sums, preferred_element_type=jnp.float32)  35.7 us
    gather x1, local copies, waits for them, and re-layouts, shards(): preact = target[:, None, :] + source[neighbours] + edge_bias  31.4 us
    reduce_sum x1, other arithmetic, shards(): messages = jnp.mean(jax.nn.gelu(preact), axis=1).astype(jnp.bfloat16)  7.74 us
    ppermute x1, starting transfers between devices, extended_2(): lax.ppermute(head, axis, [((i + 1) % count, i) for i in range(count)])  6.72 us
    all_to_all x1, starting transfers between devices, shards(): lax.all_to_all(jnp.stack([local_keys] * lax.axis_size(('grp', 'dom'))), (...  6.61 us
  transfers between devices with their start and end apart: 3, of which 1 were waited for; matrix products, arithmetic and copies ran while one was open for 2% of the time, Pallas kernels for 0%

profile of v1, /device:TPU:0, one launch (start us, length us, event | category | flops | bytes accessed | tf_op | source)
XLA Modules:
  0.0 313.6 jit_solution(11008944966914575057)
XLA Ops:
  0.6 0.8 compare_select_fusion.3
  1.4 1.9 gather_fusion
  3.3 1.6 collective-permute-start
  4.9 1.9 gather_fusion.1
  6.8 6.7 %collective-permute-start.1 = (bf16[128,256]{1,0:T(8,128)(2,1)S(1)}, bf16[128,256]{1,0:T(8,128)(2,1)}, u32[]{:S(2)}, u32[]{:S(2)}) collective-permute-start(bf16[128,256]{1,0:T(8,128)(2,1)S(1)} %gather_fusion.1), channel_id=1, source_target_pairs={{1,0},{2,1},{3,2},{4,3},{5,4},{6,5},{7,6},{8,7},{9,8},{10,9},{11,1... | collective-permute-start | bytes 196616 | tf_op jit(solution)/shard_map/ppermute | solution.py:17
  13.5 1.2 copy.18
  14.8 0.8 compare_select_fusion
  15.5 0.2 copy.19
  15.7 0.3 reshape.50
  16.0 1.4 fusion.46
  17.4 0.7 compare_select_fusion.1
  18.1 0.6 copy-done.7
  18.7 1.4 fusion.36
  20.1 31.4 %gather_fusion.2 = f32[8192,256]{1,0:T(8,128)} fusion(f32[1280,256]{1,0:T(8,128)S(1)} %fusion.36, s32[8192]{0:T(1024)S(1)} %broadcast_clamp_fusion), kind=kCustom, calls=%fused_computation.2 | custom fusion | bytes 16809984 | tf_op jit(solution)/shard_map/gather | solution.py:87
  51.6 7.7 %fusion.30 = f32[1024,256]{1,0:T(8,128)S(1)} fusion(f32[8192,256]{1,0:T(8,128)} %gather_fusion.2, f32[256]{0:T(256)S(1)} %copy-done.8, f32[1024,256]{1,0:T(8,128)S(1)} %fusion.46), kind=kLoop, calls=%fused_computation.31 | loop fusion | flops 22806528 | bytes 10486784 | tf_op jit(solution)/shard_map/reduce_sum | solution.py:88
  59.3 0.4 fusion.34
  59.8 0.1 fusion.35
  59.9 0.2 copy.20
  60.1 0.7 gather_fusion.3
  60.8 0.1 convolution_convert_fusion.2
  60.9 2.5 stack.2
  63.4 6.6 %all-to-all-start = ((bf16[128,64,256]{2,1,0:T(8,128)(2,1)}), bf16[128,64,256]{2,1,0:T(8,128)(2,1)}, u32[]{:S(2)}, u32[]{:S(2)}) async-start(bf16[128,64,256]{2,1,0:T(8,128)(2,1)} %stack.2), calls=%async_computation | async-start | bytes 8388608 | tf_op jit(solution)/shard_map/all_to_all | solution.py:99
  70.1 0.4 convolution_convert_fusion.1
  70.4 0.4 convolution_convert_fusion
  70.8 52.0 %all-to-all-done = bf16[128,64,256]{2,1,0:T(8,128)(2,1)} async-done(((bf16[128,64,256]{2,1,0:T(8,128)(2,1)}), bf16[128,64,256]{2,1,0:T(8,128)(2,1)}, u32[]{:S(2)}, u32[]{:S(2)}) %all-to-all-start) | async-done | bytes 4194336 | tf_op jit(solution)/shard_map/all_to_all | solution.py:99
  122.8 41.6 %while.21 = (s32[]{:T(128)}, f32[16,512,256]{2,1,0:T(8,128)}, bf16[16,512,256]{2,1,0:T(8,128)(2,1)}, bf16[1024,256]{1,0:T(8,128)(2,1)S(1)}, bf16[1024,256]{1,0:T(8,128)(2,1)S(1)}, /*index=5*/s32[]{:T(128)}) while((s32[]{:T(128)}, f32[16,512,256]{2,1,0:T(8,128)}, bf16[16,512,256]{2,1,0:T(8,128)(2,1)}, bf16[1024,256]{1,0:T(8,128)(2,1)S(1)}, ...), condition=%wide.region_3.4_spmd, body=%wide.region_2.3_spmd.sunk | while | flops 537919488 | bytes 1836101 | solution.py:46
  122.8 2.6 fusion.72
  125.4 2.6 fusion.72
  128.0 2.6 fusion.72
  130.6 2.6 fusion.72
  133.2 2.6 fusion.72
  135.8 2.6 fusion.72
  138.4 2.6 fusion.72
  141.0 2.6 fusion.72
  143.6 2.6 fusion.72
  146.2 2.6 fusion.72
  148.8 2.6 fusion.72
  151.4 2.6 fusion.72
  154.0 2.6 fusion.72
  156.6 2.6 fusion.72
  159.2 2.6 fusion.72
  161.8 2.6 fusion.72
  164.4 111.3 %all-reduce.1 = bf16[8192,256]{1,0:T(8,128)(2,1)} all-reduce(f32[8192,256]{1,0:T(8,128)} %bitcast.52), channel_id=1, replica_groups=mesh['grp'=4,'dom'=32] {'grp','dom'}, use_global_device_ids=true, to_apply=%region_4.5 | all-reduce | flops 2097152 | bytes 12582912 | tf_op jit(solution)/shard_map/psum | solution.py:105
  275.7 36.1 %while.22 = (s32[]{:T(128)}, f32[1024,256]{1,0:T(8,128)S(1)}, bf16[16,512,256]{2,1,0:T(8,128)(2,1)}, bf16[1024,256]{1,0:T(8,128)(2,1)S(1)}, bf16[16,512,256]{2,1,0:T(8,128)(2,1)}, /*index=5*/s32[]{:T(128)}, s32[]{:T(128)}) while((s32[]{:T(128)}, f32[1024,256]{1,0:T(8,128)S(1)}, bf16[16,512,256]{2,1,0:T(8,128)(2,1)}, ...), condition=%wide.region_6.7_spmd.clone, body=%wide.region_5.6_spmd.clone.sunk | while | flops 538443776 | bytes 3146839 | solution.py:61
  275.7 2.3 fusion.76
  278.0 2.2 fusion.76
  280.3 2.2 fusion.76
  282.5 2.2 fusion.76
  284.8 2.2 fusion.76
  287.0 2.2 fusion.76
  289.3 2.2 fusion.76
  291.5 2.2 fusion.76
  293.8 2.2 fusion.76
  296.0 2.2 fusion.76
  298.3 2.2 fusion.76
  300.5 2.2 fusion.76
  302.8 2.2 fusion.76
  305.1 2.2 fusion.76
  307.3 2.2 fusion.76
  309.6 2.2 fusion.76
  311.8 0.2 multiply_reduce_fusion
  312.0 0.2 broadcast_multiply_fusion
  312.3 0.3 fusion.32
  312.6 1.0 copy.22
  (27 shorter events, 0.1 us)
Async XLA Ops:
  0.6 18.1 %copy-start = (bf16[256,256]{1,0:T(8,128)(2,1)S(1)}, bf16[256,256]{1,0:T(8,128)(2,1)}, u32[]{:S(2)}) copy-start(bf16[256,256]{1,0:T(8,128)(2,1)} %param.21) | copy-start | bytes 393220
  3.3 14.8 %collective-permute-start = (bf16[128,256]{1,0:T(8,128)(2,1)S(1)}, bf16[128,256]{1,0:T(8,128)(2,1)S(1)}, u32[]{:S(2)}, u32[]{:S(2)}) collective-permute-start(bf16[128,256]{1,0:T(8,128)(2,1)S(1)} %gather_fusion), channel_id=1, source_target_pairs={{0,1},{1,2},{2,3},{3,4},{4,5},{5,6},{6,7},{7,8},{8,9},{9,10},{10,1... | collective-permute-start | bytes 196616 | tf_op jit(solution)/shard_map/ppermute | solution.py:15
  6.8 11.9 %collective-permute-start.1 = (bf16[128,256]{1,0:T(8,128)(2,1)S(1)}, bf16[128,256]{1,0:T(8,128)(2,1)}, u32[]{:S(2)}, u32[]{:S(2)}) collective-permute-start(bf16[128,256]{1,0:T(8,128)(2,1)S(1)} %gather_fusion.1), channel_id=1, source_target_pairs={{1,0},{2,1},{3,2},{4,3},{5,4},{6,5},{7,6},{8,7},{9,8},{10,9},{11,1... | collective-permute-start | bytes 196616 | tf_op jit(solution)/shard_map/ppermute | solution.py:17
  18.0 0.6 copy-start.7
  20.1 31.4 %copy-start.8 = (f32[256]{0:T(256)S(1)}, f32[256]{0:T(256)}, u32[]{:S(2)}) copy-start(f32[256]{0:T(256)} %param.23) | copy-start | bytes 3076
  51.6 7.8 %copy-start.2 = (bf16[256,256]{1,0:T(8,128)(2,1)S(1)}, bf16[256,256]{1,0:T(8,128)(2,1)}, u32[]{:S(2)}) copy-start(bf16[256,256]{1,0:T(8,128)(2,1)} %param.22) | copy-start | bytes 393220
  51.6 9.2 %copy-start.6 = (bf16[256,256]{1,0:T(8,128)(2,1)S(1)}, bf16[256,256]{1,0:T(8,128)(2,1)}, u32[]{:S(2)}) copy-start(bf16[256,256]{1,0:T(8,128)(2,1)} %param.25) | copy-start | bytes 393220
  59.3 10.7 %copy-start.3 = (bf16[256,256]{1,0:T(8,128)(2,1)S(1)}, bf16[256,256]{1,0:T(8,128)(2,1)}, u32[]{:S(2)}) copy-start(bf16[256,256]{1,0:T(8,128)(2,1)} %param.24) | copy-start | bytes 393220
  59.7 10.7 %copy-start.4 = (bf16[256,256]{1,0:T(8,128)(2,1)S(1)}, bf16[256,256]{1,0:T(8,128)(2,1)}, u32[]{:S(2)}) copy-start(bf16[256,256]{1,0:T(8,128)(2,1)} %param.26) | copy-start | bytes 393220
  63.4 59.4 %all-to-all-start = ((bf16[128,64,256]{2,1,0:T(8,128)(2,1)}), bf16[128,64,256]{2,1,0:T(8,128)(2,1)}, u32[]{:S(2)}, u32[]{:S(2)}) async-start(bf16[128,64,256]{2,1,0:T(8,128)(2,1)} %stack.2), calls=%async_computation | async-start | bytes 8388608 | tf_op jit(solution)/shard_map/all_to_all | solution.py:99
  275.7 36.5 %copy-start.5 = (bf16[256,256]{1,0:T(8,128)(2,1)S(1)}, bf16[256,256]{1,0:T(8,128)(2,1)}, u32[]{:S(2)}) copy-start(bf16[256,256]{1,0:T(8,128)(2,1)} %param.27) | copy-start | bytes 393220
  312.3 1.4 copy-start.1
